TPU v7x, 32 devices: a whole 2x2x4 slice. The times are simulated.
32 devices in a mesh: tile: 4 (over x, core), blk: 8 (over z, y).
Axes of the slice: x: 2, y: 2, z: 4, core: 2. Of those that a mesh axis runs over, the one named last changes fastest.
Arguments:
- tokens: bfloat16 [32768, 384], P(('tile', 'blk')), may hold values from -52 to 52
- ln_gain: float32 [384], replicated, may hold values from 0.1 to 1.9
- route: int32 [32768, 2], P(('tile', 'blk')), may hold values from 0 to 15, all different within a row; in each aligned block of 1024 rows (0 to 1023, 1024 to 2047, ...) at most 192 rows name the same one
- gates: float32 [32768, 2], P(('tile', 'blk')), may hold values from 0.1 to 1
- w_gate: bfloat16 [16, 384, 1024], P('tile', 'blk'), may hold values from -0.3125 to 0.3125
- w_up: bfloat16 [16, 384, 1024], P('tile', 'blk'), may hold values from -0.3125 to 0.3125
- w_down: bfloat16 [16, 1024, 384], P('tile', 'blk'), may hold values from -0.1875 to 0.1875
- d_mixed: bfloat16 [32768, 384], P(('tile', 'blk')), may hold values from -6 to 6
Outputs:
- mixed: bfloat16 [32768, 384], P(('tile', 'blk'))
- grad_gates: float32 [32768, 2], P(('tile', 'blk'))
- grad_tokens: bfloat16 [32768, 384], P(('tile', 'blk'))
- grad_w_gate: float32 [16, 384, 1024], P('tile', 'blk')
- grad_w_up: float32 [16, 384, 1024], P('tile', 'blk')
- grad_w_down: float32 [16, 1024, 384], P('tile', 'blk')
Inputs may be any that keep to these rules, and one draw needn't show every extreme that they name: `route`: each row names 2 different experts; within the rows of one device no expert is named more than 192 times, a bound that some block reaches.
All inputs are finite; a program needn't handle non-finite values.
Results may differ from a plain program's by a relative error of at most 0.014.
Values may be sent and summed in bfloat16 or wider, within the bound.
A program may use at most 192 MiB of HBM per device.

v0:
```python
import jax
import jax.numpy as jnp
from jax import lax
from jax.sharding import PartitionSpec as P


def layer_norm(values, ln_gain):
    centre = jnp.mean(values, axis=-1, keepdims=True)
    centred = values - centre
    spread = jnp.mean(centred * centred, axis=-1, keepdims=True)
    return values * lax.rsqrt(spread + 1e-05) * ln_gain


def expert_forward(inputs_rows, weight_gate, weight_up, weight_down):
    gate_pre = jnp.einsum(
        "erd,edh->erh", inputs_rows, weight_gate, preferred_element_type=jnp.float32
    )
    up_pre = jnp.einsum("erd,edh->erh", inputs_rows, weight_up, preferred_element_type=jnp.float32)
    sigma_gate = jax.nn.sigmoid(gate_pre)
    hidden_act = (gate_pre * sigma_gate * up_pre).astype(jnp.bfloat16)
    expert_rows = jnp.einsum(
        "erh,ehd->erd", hidden_act, weight_down, preferred_element_type=jnp.float32
    )
    return (expert_rows.astype(jnp.bfloat16), gate_pre, up_pre, hidden_act)


def expert_backward(
    inputs_rows, d_rows, gate_pre, up_pre, hidden_act, weight_gate, weight_up, weight_down
):
    d_act = jnp.einsum("erd,ehd->erh", d_rows, weight_down, preferred_element_type=jnp.float32)
    sigma_gate = jax.nn.sigmoid(gate_pre)
    d_gate = (d_act * up_pre * sigma_gate * (1.0 + gate_pre * (1.0 - sigma_gate))).astype(
        jnp.bfloat16
    )
    d_up = (d_act * gate_pre * sigma_gate).astype(jnp.bfloat16)
    d_in = jnp.einsum(
        "erh,edh->erd", d_gate, weight_gate, preferred_element_type=jnp.float32
    ) + jnp.einsum("erh,edh->erd", d_up, weight_up, preferred_element_type=jnp.float32)
    grad_gate = jnp.einsum("erd,erh->edh", inputs_rows, d_gate, preferred_element_type=jnp.float32)
    grad_up = jnp.einsum("erd,erh->edh", inputs_rows, d_up, preferred_element_type=jnp.float32)
    grad_down = jnp.einsum("erh,erd->ehd", hidden_act, d_rows, preferred_element_type=jnp.float32)
    return (d_in.astype(jnp.bfloat16), grad_gate, grad_up, grad_down)


def on_device(tokens, ln_gain, route, gates, w_gate, w_up, w_down, d_mixed):
    tok_rows, features = tokens.shape
    top_picks = route.shape[1]
    per_tile = w_gate.shape[0]
    tile_count = lax.axis_size("tile")
    experts_all = per_tile * tile_count
    capacity = max(2, 3 * tok_rows * top_picks // (2 * experts_all))
    tokens_wide = tokens.astype(jnp.float32)
    normed = layer_norm(tokens_wide, ln_gain).astype(jnp.bfloat16)
    flat_route = route.reshape(-1)
    onehot = (flat_route[:, None] == lax.iota(jnp.int32, experts_all)[None, :]).astype(jnp.int32)
    slot_rank = jnp.sum((jnp.cumsum(onehot, axis=0) - 1) * onehot, axis=1)
    slot_index = flat_route * capacity + slot_rank

    def pack_slots(values):
        blank = jnp.zeros((experts_all * capacity, features), jnp.bfloat16)
        return blank.at[slot_index].set(values).reshape(tile_count, per_tile, capacity, features)

    def to_experts(packed):
        arrived = lax.all_to_all(packed, "tile", split_axis=0, concat_axis=2, tiled=True)[0]
        return arrived

    def from_experts(results):
        returned = lax.all_to_all(results[None], "tile", split_axis=2, concat_axis=0, tiled=True)
        picked = returned.reshape(experts_all * capacity, features)[slot_index]
        return picked.reshape(tok_rows, top_picks, features).astype(jnp.float32)

    weight_gate, weight_up, weight_down = (
        lax.all_gather(w_gate, "blk", axis=1, tiled=True),
        lax.all_gather(w_up, "blk", axis=1, tiled=True),
        lax.all_gather(w_down, "blk", axis=1, tiled=True),
    )
    inputs_rows = to_experts(pack_slots(jnp.repeat(normed, top_picks, axis=0)))
    expert_rows, gate_pre, up_pre, hidden_act = expert_forward(
        inputs_rows, weight_gate, weight_up, weight_down
    )
    expert_out = from_experts(expert_rows)
    mixed = jnp.sum(gates[:, :, None] * expert_out, axis=1).astype(jnp.bfloat16)
    d_wide = d_mixed.astype(jnp.float32)
    grad_gates = jnp.sum(d_wide[:, None, :] * expert_out, axis=-1)
    d_out = (
        (gates[:, :, None] * d_wide[:, None, :])
        .astype(jnp.bfloat16)
        .reshape(tok_rows * top_picks, features)
    )
    d_rows = to_experts(pack_slots(d_out))
    d_in, grad_gate, grad_up, grad_down = expert_backward(
        inputs_rows, d_rows, gate_pre, up_pre, hidden_act, weight_gate, weight_up, weight_down
    )
    d_normed = jnp.sum(from_experts(d_in), axis=1)

    def normalize(values):
        return layer_norm(values, ln_gain)

    unused, pullback = jax.vjp(normalize, tokens_wide)
    grad_tokens = pullback(d_normed)[0].astype(jnp.bfloat16)
    total_gate, total_up, total_down = (
        lax.psum_scatter(
            grad_gate.astype(jnp.bfloat16), "blk", scatter_dimension=1, tiled=True
        ).astype(jnp.float32),
        lax.psum_scatter(
            grad_up.astype(jnp.bfloat16), "blk", scatter_dimension=1, tiled=True
        ).astype(jnp.float32),
        lax.psum_scatter(
            grad_down.astype(jnp.bfloat16), "blk", scatter_dimension=1, tiled=True
        ).astype(jnp.float32),
    )
    return (mixed, grad_gates, grad_tokens, total_gate, total_up, total_down)


def solution(mesh):
    placed = (
        P(("tile", "blk"), None),
        P(),
        P(("tile", "blk"), None),
        P(("tile", "blk"), None),
        P("tile", "blk", None),
        P("tile", "blk", None),
        P("tile", "blk", None),
        P(("tile", "blk"), None),
    )
    return jax.shard_map(
        on_device,
        mesh=mesh,
        in_specs=placed,
        out_specs=(
            P(("tile", "blk"), None),
            P(("tile", "blk"), None),
            P(("tile", "blk"), None),
            P("tile", "blk", None),
            P("tile", "blk", None),
            P("tile", "blk", None),
        ),
        check_vma=False,
    )
```

profile of v0, /device:TPU:0, one launch (start us, length us, event | category | flops | bytes accessed | tf_op | source)
XLA Modules:
  0.0 456.1 jit_solution(16825820951956494859)
XLA Ops:
  7.2 0.7 all-gather.4.cloned.1.call-update
  8.0 0.7 all-gather.6.cloned.1.call-update
  8.7 0.7 all-gather.8.cloned.1.call-update
  9.4 0.9 copy.34
  10.3 0.3 eq.29
  10.6 4.6 reduce-window.6
  15.2 0.4 slice_reduce_fusion
  16.1 0.5 fusion.3
  16.6 0.3 fusion.10
  16.9 0.3 eq.25
  17.4 0.3 mul.136
  17.7 0.8 broadcast_in_dim.10
  18.5 1.5 reshape.153
  20.1 11.6 %scatter_custom_fusion = bf16[3072,384]{1,0:T(8,128)(2,1)} fusion(s32[2048]{0:T(1024)S(1)} %bitcast.70, bf16[2048,384]{1,0:T(8,128)(2,1)} %reshape.153, bf16[]{:T(256)} %constant.10.clone.1), kind=kCustom, calls=%fused_computation.35 | custom fusion | bytes 2359808 | tf_op jit(solution)/shard_map/scatter | solution.py:61
  31.7 4.5 all-to-all-start
  36.2 1.0 copy.32
  37.3 1.3 mul.148
  38.6 3.6 mul.146
  42.2 5.4 %mul.150 = f32[2048,384]{1,0:T(8,128)} reshape(f32[1024,2,384]{2,1,0:T(2,128)} %mul.146) | data formatting | bytes 6291456 | tf_op jit(solution)/shard_map/mul | solution.py:84
  47.6 12.6 %scatter_custom_fusion.1 = bf16[3072,384]{1,0:T(8,128)(2,1)} fusion(s32[2048]{0:T(1024)S(1)} %bitcast.71, f32[2048,384]{1,0:T(8,128)} %mul.150, f32[2048]{0:T(1024)S(1)} %mul.148, bf16[]{:T(256)} %constant.10.clone.1), kind=kCustom, calls=%fused_computation.32 | custom fusion | flops 1572864 | bytes 5513218 | tf_op jit(solution)/shard_map/scatter | solution.py:61
  60.2 4.6 %all-to-all-done = bf16[4,4,192,384]{3,2,1,0:T(8,128)(2,1)S(1)} async-done(((bf16[4,4,192,384]{3,2,1,0:T(8,128)(2,1)}), bf16[4,4,192,384]{3,2,1,0:T(8,128)(2,1)S(1)}, u32[]{:S(2)}, u32[]{:S(2)}) %all-to-all-start) | async-done | bytes 2359328 | tf_op jit(solution)/shard_map/all_to_all | solution.py:64
  64.8 1.4 copy-done.1
  66.2 4.5 all-to-all-start.2
  70.9 1.9 copy.36
  72.9 26.3 %all-to-all-done.2 = bf16[4,4,192,384]{3,2,1,0:T(8,128)(2,1)} async-done(((bf16[4,4,192,384]{3,2,1,0:T(8,128)(2,1)}), bf16[4,4,192,384]{3,2,1,0:T(8,128)(2,1)}, u32[]{:S(2)}, u32[]{:S(2)}) %all-to-all-start.2) | async-done | bytes 2359328 | tf_op jit(solution)/shard_map/all_to_all | solution.py:64
  99.2 3.4 copy.40
  102.6 8.7 %fusion.21 = f32[4,768,1024]{2,1,0:T(8,128)} fusion(bf16[4,768,384]{2,1,0:T(8,128)(2,1)S(1)} %bitcast.58, bf16[4,384,1024]{2,1,0:T(8,128)(2,1)} %all-gather.4.cloned.1.call-done), kind=kOutput, calls=%fused_computation.53 | convolution fusion | flops 2415919104 | bytes 18087936 | tf_op jit(solution)/shard_map/erd,edh->erh/dot_general | solution.py:15
  111.3 22.6 %all-gather.6.cloned.1.call-done = bf16[4,384,1024]{2,1,0:T(8,128)(2,1)} async-done(((bf16[4,48,1024]{2,1,0:T(8,128)(2,1)}), bf16[4,384,1024]{2,1,0:T(8,128)(2,1)}) %all-gather.6.cloned.1.call-update) | async-done | bytes 3145744 | tf_op jit(solution)/shard_map/all_gather | solution.py:74
  133.9 8.3 %fusion.22 = f32[4,768,1024]{2,1,0:T(8,128)} fusion(bf16[4,768,384]{2,1,0:T(8,128)(2,1)S(1)} %bitcast.59, bf16[4,384,1024]{2,1,0:T(8,128)(2,1)} %all-gather.6.cloned.1.call-done), kind=kOutput, calls=%fused_computation.54 | convolution fusion | flops 2415919104 | bytes 18087936 | tf_op jit(solution)/shard_map/erd,edh->erh/dot_general | solution.py:18
  142.2 52.6 %all-gather.8.cloned.1.call-done = bf16[4,1024,384]{2,1,0:T(8,128)(2,1)} async-done(((bf16[4,128,384]{2,1,0:T(8,128)(2,1)}), bf16[4,1024,384]{2,1,0:T(8,128)(2,1)}) %all-gather.8.cloned.1.call-update) | async-done | bytes 3145744 | tf_op jit(solution)/shard_map/all_gather | solution.py:75
  194.8 18.0 %multiply_convert_fusion = (bf16[4,768,1024]{2,1,0:T(8,128)(2,1)}, bf16[4,768,1024]{2,1,0:T(8,128)(2,1)}, bf16[4,768,1024]{2,1,0:T(8,128)(2,1)}) fusion(f32[4,768,1024]{2,1,0:T(8,128)} %fusion.21, f32[4,768,1024]{2,1,0:T(8,128)} %fusion.22, bf16[4,768,384]{2,1,0:T(8,128)(2,1)} %bitcast.66, bf16[4,1024,384]{2,1,0:T(8,128)(2,1)} %all-gather.8.cloned.1.call-done), kind=kOutput, calls=%fused_computation.4 | convolution fusion | flops 2466250752 | bytes 49545216 | tf_op jit(solution)/shard_map/erd,ehd->erh/dot_general | solution.py:30
  212.8 7.1 %convolution_convert_fusion.2 = bf16[4,384,1024]{2,1,0:T(8,128)(2,1)} fusion(bf16[4,768,384]{2,1,0:T(8,128)(2,1)S(1)} %bitcast.60, bf16[4,768,1024]{2,1,0:T(8,128)(2,1)} %get-tuple-element.15), kind=kOutput, calls=%fused_computation.20 | convolution fusion | flops 2417491968 | bytes 11796480 | tf_op jit(solution)/shard_map/erd,erh->edh/dot_general | solution.py:39
  219.9 0.5 reduce-scatter.6.cloned.1.call-start
  220.5 7.1 %convolution_convert_fusion.1 = bf16[4,384,1024]{2,1,0:T(8,128)(2,1)} fusion(bf16[4,768,384]{2,1,0:T(8,128)(2,1)S(1)} %bitcast.61, bf16[4,768,1024]{2,1,0:T(8,128)(2,1)} %get-tuple-element.14), kind=kOutput, calls=%fused_computation.19 | convolution fusion | flops 2417491968 | bytes 11796480 | tf_op jit(solution)/shard_map/erd,erh->edh/dot_general | solution.py:40
  227.7 1.6 copy-done.7
  229.3 8.0 %convolution_convert_fusion = bf16[4,1024,384]{2,1,0:T(8,128)(2,1)} fusion(bf16[4,768,1024]{2,1,0:T(8,128)(2,1)} %get-tuple-element.16, bf16[4,768,384]{2,1,0:T(8,128)(2,1)S(1)} %bitcast.67), kind=kOutput, calls=%fused_computation.18 | convolution fusion | flops 2417491968 | bytes 11796480 | tf_op jit(solution)/shard_map/erh,erd->ehd/dot_general | solution.py:41
  237.3 6.7 %fusion.23 = f32[4,768,384]{2,1,0:T(8,128)S(1)} fusion(bf16[4,768,1024]{2,1,0:T(8,128)(2,1)} %get-tuple-element.15, bf16[4,384,1024]{2,1,0:T(8,128)(2,1)} %all-gather.4.cloned.1.call-done), kind=kOutput, calls=%fused_computation.55 | convolution fusion | flops 2415919104 | bytes 14155776 | tf_op jit(solution)/shard_map/erh,edh->erd/dot_general | solution.py:36
  244.1 3.7 fusion
  247.8 3.2 copy.41
  251.0 3.6 all-to-all-start.3
  254.7 7.2 %convert_bitcast_fusion = bf16[1,4,768,384]{3,2,1,0:T(8,128)(2,1)S(1)} fusion(bf16[4,768,1024]{2,1,0:T(8,128)(2,1)} %get-tuple-element.16, bf16[4,1024,384]{2,1,0:T(8,128)(2,1)} %all-gather.8.cloned.1.call-done), kind=kOutput, calls=%fused_computation.17 | convolution fusion | flops 2417098752 | bytes 11796480 | tf_op jit(solution)/shard_map/erh,ehd->erd/dot_general | solution.py:21
  261.9 3.3 copy.37
  265.1 18.0 %all-to-all-done.3 = bf16[1,4,768,384]{3,1,0,2:T(4,128)(2,1)S(1)} async-done(((bf16[1,4,768,384]{3,1,0,2:T(4,128)(2,1)}), bf16[1,4,768,384]{3,1,0,2:T(4,128)(2,1)S(1)}, u32[]{:S(2)}, u32[]{:S(2)}) %all-to-all-start.3) | async-done | bytes 2359328 | tf_op jit(solution)/shard_map/all_to_all | solution.py:68
  283.1 1.4 copy-done.2
  284.5 4.7 %all-to-all-start.1 = ((bf16[1,4,768,384]{3,1,0,2:T(4,128)(2,1)}), bf16[1,4,768,384]{3,1,0,2:T(4,128)(2,1)}, u32[]{:S(2)}, u32[]{:S(2)}) async-start(bf16[1,4,768,384]{3,1,0,2:T(4,128)(2,1)} %copy.37), calls=%async_computation.1 | async-start | bytes 4718592 | tf_op jit(solution)/shard_map/all_to_all | solution.py:68
  289.2 2.6 convert_element_type.81
  291.8 0.4 copy.42
  292.2 9.0 %gather_fusion.1 = bf16[2048,384]{1,0:T(8,128)(2,1)} fusion(bf16[3072,384]{1,0:T(8,128)(2,1)S(1)} %bitcast.57, s32[2048]{0:T(1024)S(1)} %broadcast_clamp_fusion), kind=kCustom, calls=%fused_computation.1 | custom fusion | bytes 3153920 | tf_op jit(solution)/shard_map/gather | solution.py:69
  301.2 4.9 %reshape.132 = f32[1024,2,384]{2,1,0:T(2,128)} reshape(bf16[2048,384]{1,0:T(8,128)(2,1)} %gather_fusion.1) | data formatting | bytes 4718592 | tf_op jit(solution)/shard_map/convert_element_type | solution.py:70
  306.1 11.6 %all-to-all-done.1 = bf16[1,4,768,384]{3,1,0,2:T(4,128)(2,1)} async-done(((bf16[1,4,768,384]{3,1,0,2:T(4,128)(2,1)}), bf16[1,4,768,384]{3,1,0,2:T(4,128)(2,1)}, u32[]{:S(2)}, u32[]{:S(2)}) %all-to-all-start.1) | async-done | bytes 2359328 | tf_op jit(solution)/shard_map/all_to_all | solution.py:68
  317.7 2.1 copy.38
  319.9 9.1 %gather_fusion = bf16[2048,384]{1,0:T(8,128)(2,1)} fusion(bf16[3072,384]{1,0:T(8,128)(2,1)S(1)} %bitcast.56, s32[2048]{0:T(1024)S(1)} %broadcast_clamp_fusion), kind=kCustom, calls=%fused_computation | custom fusion | bytes 3153920 | tf_op jit(solution)/shard_map/gather | solution.py:69
  328.9 5.0 %reshape.131 = f32[1024,2,384]{2,1,0:T(2,128)} reshape(bf16[2048,384]{1,0:T(8,128)(2,1)} %gather_fusion) | data formatting | bytes 4718592 | tf_op jit(solution)/shard_map/convert_element_type | solution.py:70
  334.0 10.1 %multiply_reduce_fusion = (f32[1024,2]{1,0:T(8,128)S(1)}, bf16[1024,384]{1,0:T(8,128)(2,1)}) fusion(f32[1024,2,384]{2,1,0:T(2,128)} %reshape.131, f32[1024,384]{1,0:T(8,128)S(1)} %copy-done.4, f32[1024,2]{1,0:T(8,128)S(1)} %copy-done.5), kind=kLoop, calls=%fused_computation.10 | loop fusion | flops 2750464 | bytes 5521408 | tf_op jit(solution)/shard_map/reduce_sum | solution.py:84
  344.1 0.8 copy.46
  344.9 5.7 %reduce_sum.96 = f32[1024,384]{1,0:T(8,128)S(1)} reduce(f32[1024,2,384]{2,1,0:T(2,128)} %reshape.132, f32[]{:T(128)} %constant.25.clone.1), dimensions={1}, to_apply=%region_9.10 | reduce | flops 393216 | bytes 4718596 | tf_op jit(solution)/shard_map/reduce_sum | solution.py:94
  350.5 0.3 fusion.11
  350.8 0.5 fusion.5
  351.3 1.7 fusion.8
  353.0 2.0 convert_element_type.90
  355.0 15.0 %reduce-scatter.6.cloned.1.call-done = bf16[4,48,1024]{2,1,0:T(8,128)(2,1)} async-done(((bf16[4,384,1024]{2,1,0:T(8,128)(2,1)}), bf16[4,48,1024]{2,1,0:T(8,128)(2,1)}) %reduce-scatter.6.cloned.1.call-update) | async-done | bytes 393232 | tf_op jit(solution)/shard_map/reduce_scatter | solution.py:105
  370.0 2.0 convert_element_type.92
  372.0 75.1 %reduce-scatter.8.cloned.1.call-done = bf16[4,128,384]{2,1,0:T(8,128)(2,1)} async-done(((bf16[4,1024,384]{2,1,0:T(8,128)(2,1)}), bf16[4,128,384]{2,1,0:T(8,128)(2,1)}) %reduce-scatter.8.cloned.1.call-update) | async-done | bytes 393232 | tf_op jit(solution)/shard_map/reduce_scatter | solution.py:108
  447.1 1.9 convert_element_type.94
  (47 shorter events, 1.5 us)
Async XLA Ops:
  7.2 8.7 %copy-start = (bf16[1024,384]{1,0:T(8,128)(2,1)S(1)}, bf16[1024,384]{1,0:T(8,128)(2,1)}, u32[]{:S(2)}) copy-start(bf16[1024,384]{1,0:T(8,128)(2,1)} %param.8) | copy-start | bytes 2359300
  7.2 9.4 %copy-start.9 = (f32[384]{0:T(512)S(1)}, f32[384]{0:T(512)}, u32[]{:S(2)}) copy-start(f32[384]{0:T(512)} %param.9) | copy-start | bytes 4612
  7.2 95.4 %all-gather.4.cloned.1.call-start = ((), (), s32[]{:S(2)}) async-start(), calls=%async_computation.7 | async-start | bytes 3538944 | tf_op jit(solution)/shard_map/all_gather | solution.py:73
  7.9 126.0 %all-gather.6.cloned.1.call-start = ((), (), s32[]{:S(2)}) async-start(), calls=%async_computation.8 | async-start | bytes 3538944 | tf_op jit(solution)/shard_map/all_gather | solution.py:74
  8.7 186.1 %all-gather.8.cloned.1.call-start = ((), (), s32[]{:S(2)}) async-start(), calls=%async_computation.9 | async-start | bytes 3538944 | tf_op jit(solution)/shard_map/all_gather | solution.py:75
  10.3 6.5 %copy-start.8 = (s32[1024,2]{0,1:T(2,128)S(1)}, s32[1024,2]{0,1:T(2,128)}, u32[]{:S(2)}) copy-start(s32[1024,2]{0,1:T(2,128)} %param.10) | copy-start | bytes 24580
  31.7 4.5 copy-start.10
  31.7 33.1 %all-to-all-start = ((bf16[4,4,192,384]{3,2,1,0:T(8,128)(2,1)}), bf16[4,4,192,384]{3,2,1,0:T(8,128)(2,1)S(1)}, u32[]{:S(2)}, u32[]{:S(2)}) async-start(bf16[4,4,192,384]{3,2,1,0:T(8,128)(2,1)} %bitcast.65), calls=%async_computation | async-start | bytes 4718592 | tf_op jit(solution)/shard_map/all_to_all | solution.py:64
  64.8 1.4 copy-start.1
  66.2 33.0 %all-to-all-start.2 = ((bf16[4,4,192,384]{3,2,1,0:T(8,128)(2,1)}), bf16[4,4,192,384]{3,2,1,0:T(8,128)(2,1)}, u32[]{:S(2)}, u32[]{:S(2)}) async-start(bf16[4,4,192,384]{3,2,1,0:T(8,128)(2,1)} %bitcast.64), calls=%async_computation.2 | async-start | bytes 4718592 | tf_op jit(solution)/shard_map/all_to_all | solution.py:64
  70.7 282.4 %reduce-scatter.4.cloned.1.call-start = ((), (), s32[]{:S(2)}) async-start(), calls=%async_computation.10 | async-start | bytes 3538944 | tf_op jit(solution)/shard_map/reduce_scatter | solution.py:102
  219.9 150.1 %reduce-scatter.6.cloned.1.call-start = ((), (), s32[]{:S(2)}) async-start(), calls=%async_computation.11 | async-start | bytes 3538944 | tf_op jit(solution)/shard_map/reduce_scatter | solution.py:105
  227.6 1.7 copy-start.7
  227.6 219.5 %reduce-scatter.8.cloned.1.call-start = ((), (), s32[]{:S(2)}) async-start(), calls=%async_computation.12 | async-start | bytes 3538944 | tf_op jit(solution)/shard_map/reduce_scatter | solution.py:108
  237.2 6.7 %slice-start = ((s8[6291456]{0:T(1024)(128)(4,1)}), s8[2097152]{0:T(1024)(128)(4,1)S(1)}, s32[]{:S(2)}) async-start(s8[6291456]{0:T(1024)(128)(4,1)} %bitcast.74), calls=%async_computation.13 | async-start | bytes 4194304
  237.2 6.7 %copy-start.6 = (bf16[4,384,1024]{2,1,0:T(8,128)(2,1)S(1)}, bf16[4,384,1024]{2,1,0:T(8,128)(2,1)}, u32[]{:S(2)}) copy-start(bf16[4,384,1024]{2,1,0:T(8,128)(2,1)} %all-gather.6.cloned.1.call-done) | copy-start | bytes 9437188
  237.2 6.8 %slice-start.1 = ((s8[6291456]{0:T(1024)(128)(4,1)}), s8[4194304]{0:T(1024)(128)(4,1)S(1)}, s32[]{:S(2)}) async-start(s8[6291456]{0:T(1024)(128)(4,1)} %bitcast.74), calls=%async_computation.14 | async-start | bytes 8388608
  251.0 32.1 %all-to-all-start.3 = ((bf16[1,4,768,384]{3,1,0,2:T(4,128)(2,1)}), bf16[1,4,768,384]{3,1,0,2:T(4,128)(2,1)S(1)}, u32[]{:S(2)}, u32[]{:S(2)}) async-start(bf16[1,4,768,384]{3,1,0,2:T(4,128)(2,1)} %copy.41), calls=%async_computation.3 | async-start | bytes 4718592 | tf_op jit(solution)/shard_map/all_to_all | solution.py:68
  283.1 1.4 copy-start.2
  284.5 33.2 %all-to-all-start.1 = ((bf16[1,4,768,384]{3,1,0,2:T(4,128)(2,1)}), bf16[1,4,768,384]{3,1,0,2:T(4,128)(2,1)}, u32[]{:S(2)}, u32[]{:S(2)}) async-start(bf16[1,4,768,384]{3,1,0,2:T(4,128)(2,1)} %copy.37), calls=%async_computation.1 | async-start | bytes 4718592 | tf_op jit(solution)/shard_map/all_to_all | solution.py:68
  289.2 2.6 copy-start.3
  328.9 5.0 %copy-start.4 = (f32[1024,384]{1,0:T(8,128)S(1)}, f32[1024,384]{1,0:T(8,128)}, u32[]{:S(2)}) copy-start(f32[1024,384]{1,0:T(8,128)} %convert_element_type.81) | copy-start | bytes 4718596
  328.9 5.0 %copy-start.5 = (f32[1024,2]{1,0:T(8,128)S(1)}, f32[1024,2]{1,0:T(8,128)}, u32[]{:S(2)}) copy-start(f32[1024,2]{1,0:T(8,128)} %copy.32) | copy-start | bytes 24580
Sparse Core Ops, SparseCore 0:
  10.2 62.7 all-gather.3
  75.2 58.6 all-gather.5
  136.1 58.6 all-gather.7
  220.1 72.9 reduce-scatter.3
  296.5 73.4 reduce-scatter.5
  373.4 73.5 reduce-scatter.7
where the time goes:
time: 463 us; the launch traced here: 456 us
  waiting for transfers between devices  228 us (49%)
  local copies, waits for them, and re-layouts  75.3 us (16%)
  matrix products  74.9 us (16%)
  other arithmetic  45.1 us (10%)
  starting transfers between devices  18.2 us (4%)
  between operations  14.6 us (3%)
    reduce_scatter x1, waiting for transfers between devices, on_device(): lax.psum_scatter(grad_down.astype(jnp.bfloat16), 'blk', scatter_dimension...  75.1 us
    all_gather x1, waiting for transfers between devices, on_device(): lax.all_gather(w_down, 'blk', axis=1, tiled=True)  52.6 us
    all_to_all x2, waiting for transfers between devices, to_experts(): lax.all_to_all(packed, 'tile', split_axis=0, concat_axis=2, tiled=True)[0]  30.9 us
    all_to_all x2, waiting for transfers between devices, from_experts(): lax.all_to_all(results[None], 'tile', split_axis=2, concat_axis=0, tiled=...  29.6 us
    all_gather x1, waiting for transfers between devices, on_device(): lax.all_gather(w_up, 'blk', axis=1, tiled=True)  22.6 us
    gather x2, local copies, waits for them, and re-layouts, from_experts(): picked = returned.reshape(experts_all * capacity, features)[slot_index]  18.1 us
    dot_general x1, matrix products, expert_backward(): jnp.einsum('erd,ehd->erh', d_rows, weight_down, preferred_element_type=jn...  18 us
    reduce_scatter x1, waiting for transfers between devices, on_device(): lax.psum_scatter(grad_up.astype(jnp.bfloat16), 'blk', scatter_dimension=1...  15 us
  transfers between devices with their start and end apart: 10, of which 8 were waited for; matrix products, arithmetic and copies ran while one was open for 36% of the time, Pallas kernels for 0%

commit v1 on v0

--- a/solution.py
+++ b/solution.py
@@ -65,7 +65,12 @@
         return arrived
 
     def from_experts(results):
-        returned = lax.all_to_all(results[None], "tile", split_axis=2, concat_axis=0, tiled=True)
+        returned = jnp.concatenate(
+            lax.all_to_all(
+                jnp.stack(jnp.split(results[None], lax.axis_size("tile"), axis=2)), "tile", 0, 0
+            ),
+            axis=0,
+        )
         picked = returned.reshape(experts_all * capacity, features)[slot_index]
         return picked.reshape(tok_rows, top_picks, features).astype(jnp.float32)
 

time: 463 us -> 463 us (level)
  local copies, waits for them, and re-layouts: 75.3 us -> 63.2 us
  waiting for transfers between devices: 228 us -> 237 us
    reduce_scatter x1, waiting for transfers between devices: 15 us -> 21.8 us  [on_device(): lax.psum_scatter(grad_up.astype(jnp.bfloat16), 'blk', scatter_dimension=1...]
    broadcast_in_dim x2 -> x0, local copies, waits for them, and re-layouts: 6.48 us -> none  [from_experts(): results[None]]
  transfers between devices with their start and end apart: 10 -> 10, of which waited for: 8 -> 8; matrix products, arithmetic and copies ran while one was open for 36% -> 34% of each run, Pallas kernels for 0% -> 0%
where the time goes in v1:
time: 463 us; the launch traced here: 456 us
  waiting for transfers between devices  237 us (51%)
  matrix products  75 us (16%)
  local copies, waits for them, and re-layouts  63.2 us (14%)
  other arithmetic  48.7 us (11%)
  starting transfers between devices  18.2 us (4%)
  between operations  14.6 us (3%)
    reduce_scatter x1, waiting for transfers between devices, on_device(): lax.psum_scatter(grad_down.astype(jnp.bfloat16), 'blk', scatter_dimension...  75.2 us
    all_gather x1, waiting for transfers between devices, on_device(): lax.all_gather(w_down, 'blk', axis=1, tiled=True)  52.6 us
    all_to_all x2, waiting for transfers between devices, from_experts(): lax.all_to_all(jnp.stack(jnp.split(results[None], lax.axis_size('tile'),...  31.2 us
    all_to_all x2, waiting for transfers between devices, to_experts(): lax.all_to_all(packed, 'tile', split_axis=0, concat_axis=2, tiled=True)[0]  30.9 us
    all_gather x1, waiting for transfers between devices, on_device(): lax.all_gather(w_up, 'blk', axis=1, tiled=True)  22.6 us
    reduce_scatter x1, waiting for transfers between devices, on_device(): lax.psum_scatter(grad_up.astype(jnp.bfloat16), 'blk', scatter_dimension=1...  21.8 us
    gather x2, local copies, waits for them, and re-layouts, from_experts(): picked = returned.reshape(experts_all * capacity, features)[slot_index]  18.2 us
    dot_general x1, matrix products, expert_backward(): jnp.einsum('erd,ehd->erh', d_rows, weight_down, preferred_element_type=jn...  18 us
  transfers between devices with their start and end apart: 10, of which 8 were waited for; matrix products, arithmetic and copies ran while one was open for 34% of the time, Pallas kernels for 0%

profile of v1, /device:TPU:0, one launch (start us, length us, event | category | flops | bytes accessed | tf_op | source)
XLA Modules:
  0.0 456.1 jit_solution(5669090185772937729)
XLA Ops:
  7.2 0.7 all-gather.4.cloned.1.call-update
  8.0 0.7 all-gather.6.cloned.1.call-update
  8.7 0.7 all-gather.8.cloned.1.call-update
  9.4 0.9 copy.30
  10.3 0.3 eq.29
  10.6 4.6 reduce-window.6
  15.2 0.4 slice_reduce_fusion
  16.1 0.5 fusion.3
  16.6 0.3 fusion.10
  16.9 0.3 eq.25
  17.4 0.3 mul.136
  17.7 0.8 broadcast_in_dim.10
  18.5 1.5 reshape.143
  20.1 11.6 %scatter_custom_fusion = bf16[3072,384]{1,0:T(8,128)(2,1)} fusion(s32[2048]{0:T(1024)S(1)} %bitcast.78, bf16[2048,384]{1,0:T(8,128)(2,1)} %reshape.143, bf16[]{:T(256)} %constant.10.clone.1), kind=kCustom, calls=%fused_computation.37 | custom fusion | bytes 2359808 | tf_op jit(solution)/shard_map/scatter | solution.py:61
  31.7 4.5 all-to-all-start
  36.2 1.0 copy.28
  37.3 1.3 mul.148
  38.6 3.6 mul.146
  42.2 5.4 %mul.150 = f32[2048,384]{1,0:T(8,128)} reshape(f32[1024,2,384]{2,1,0:T(2,128)} %mul.146) | data formatting | bytes 6291456 | tf_op jit(solution)/shard_map/mul | solution.py:89
  47.6 12.6 %scatter_custom_fusion.1 = bf16[3072,384]{1,0:T(8,128)(2,1)} fusion(s32[2048]{0:T(1024)S(1)} %bitcast.79, f32[2048,384]{1,0:T(8,128)} %mul.150, f32[2048]{0:T(1024)S(1)} %mul.148, bf16[]{:T(256)} %constant.10.clone.1), kind=kCustom, calls=%fused_computation.34 | custom fusion | flops 1572864 | bytes 5513218 | tf_op jit(solution)/shard_map/scatter | solution.py:61
  60.2 4.6 %all-to-all-done = bf16[4,4,192,384]{3,2,1,0:T(8,128)(2,1)S(1)} async-done(((bf16[4,4,192,384]{3,2,1,0:T(8,128)(2,1)}), bf16[4,4,192,384]{3,2,1,0:T(8,128)(2,1)S(1)}, u32[]{:S(2)}, u32[]{:S(2)}) %all-to-all-start) | async-done | bytes 2359328 | tf_op jit(solution)/shard_map/all_to_all | solution.py:64
  64.8 1.4 copy-done.1
  66.2 4.5 all-to-all-start.2
  70.7 0.3 reduce-scatter.4.cloned.1.call-start
  70.9 1.9 copy.32
  72.9 26.3 %all-to-all-done.2 = bf16[4,4,192,384]{3,2,1,0:T(8,128)(2,1)} async-done(((bf16[4,4,192,384]{3,2,1,0:T(8,128)(2,1)}), bf16[4,4,192,384]{3,2,1,0:T(8,128)(2,1)}, u32[]{:S(2)}, u32[]{:S(2)}) %all-to-all-start.2) | async-done | bytes 2359328 | tf_op jit(solution)/shard_map/all_to_all | solution.py:64
  99.2 3.4 copy.34
  102.6 8.7 %fusion.21 = f32[4,768,1024]{2,1,0:T(8,128)} fusion(bf16[4,768,384]{2,1,0:T(8,128)(2,1)S(1)} %bitcast.67, bf16[4,384,1024]{2,1,0:T(8,128)(2,1)} %all-gather.4.cloned.1.call-done), kind=kOutput, calls=%fused_computation.63 | convolution fusion | flops 2415919104 | bytes 18087936 | tf_op jit(solution)/shard_map/erd,edh->erh/dot_general | solution.py:15
  111.3 22.6 %all-gather.6.cloned.1.call-done = bf16[4,384,1024]{2,1,0:T(8,128)(2,1)} async-done(((bf16[4,48,1024]{2,1,0:T(8,128)(2,1)}), bf16[4,384,1024]{2,1,0:T(8,128)(2,1)}) %all-gather.6.cloned.1.call-update) | async-done | bytes 3145744 | tf_op jit(solution)/shard_map/all_gather | solution.py:79
  133.9 8.3 %fusion.22 = f32[4,768,1024]{2,1,0:T(8,128)} fusion(bf16[4,768,384]{2,1,0:T(8,128)(2,1)S(1)} %bitcast.68, bf16[4,384,1024]{2,1,0:T(8,128)(2,1)} %all-gather.6.cloned.1.call-done), kind=kOutput, calls=%fused_computation.64 | convolution fusion | flops 2415919104 | bytes 18087936 | tf_op jit(solution)/shard_map/erd,edh->erh/dot_general | solution.py:18
  142.2 52.6 %all-gather.8.cloned.1.call-done = bf16[4,1024,384]{2,1,0:T(8,128)(2,1)} async-done(((bf16[4,128,384]{2,1,0:T(8,128)(2,1)}), bf16[4,1024,384]{2,1,0:T(8,128)(2,1)}) %all-gather.8.cloned.1.call-update) | async-done | bytes 3145744 | tf_op jit(solution)/shard_map/all_gather | solution.py:80
  194.8 18.0 %multiply_convert_fusion = (bf16[4,768,1024]{2,1,0:T(8,128)(2,1)}, bf16[4,768,1024]{2,1,0:T(8,128)(2,1)}, bf16[4,768,1024]{2,1,0:T(8,128)(2,1)}) fusion(f32[4,768,1024]{2,1,0:T(8,128)} %fusion.21, f32[4,768,1024]{2,1,0:T(8,128)} %fusion.22, bf16[4,768,384]{2,1,0:T(8,128)(2,1)} %bitcast.74, bf16[4,1024,384]{2,1,0:T(8,128)(2,1)} %all-gather.8.cloned.1.call-done), kind=kOutput, calls=%fused_computation.4 | convolution fusion | flops 2466250752 | bytes 49545216 | tf_op jit(solution)/shard_map/erd,ehd->erh/dot_general | solution.py:30
  212.8 7.1 %convolution_convert_fusion.2 = bf16[4,384,1024]{2,1,0:T(8,128)(2,1)} fusion(bf16[4,768,384]{2,1,0:T(8,128)(2,1)S(1)} %bitcast.69, bf16[4,768,1024]{2,1,0:T(8,128)(2,1)} %get-tuple-element.15), kind=kOutput, calls=%fused_computation.22 | convolution fusion | flops 2417491968 | bytes 11796480 | tf_op jit(solution)/shard_map/erd,erh->edh/dot_general | solution.py:39
  219.9 0.4 reduce-scatter.6.cloned.1.call-start
  220.4 7.1 %convolution_convert_fusion.1 = bf16[4,384,1024]{2,1,0:T(8,128)(2,1)} fusion(bf16[4,768,384]{2,1,0:T(8,128)(2,1)S(1)} %bitcast.70, bf16[4,768,1024]{2,1,0:T(8,128)(2,1)} %get-tuple-element.14), kind=kOutput, calls=%fused_computation.21 | convolution fusion | flops 2417491968 | bytes 11796480 | tf_op jit(solution)/shard_map/erd,erh->edh/dot_general | solution.py:40
  227.6 1.6 copy-done.4
  229.2 8.0 %convolution_convert_fusion = bf16[4,1024,384]{2,1,0:T(8,128)(2,1)} fusion(bf16[4,768,1024]{2,1,0:T(8,128)(2,1)} %get-tuple-element.16, bf16[4,768,384]{2,1,0:T(8,128)(2,1)S(1)} %bitcast.75), kind=kOutput, calls=%fused_computation.20 | convolution fusion | flops 2417491968 | bytes 11796480 | tf_op jit(solution)/shard_map/erh,erd->ehd/dot_general | solution.py:41
  237.2 6.7 %fusion.23 = f32[4,768,384]{2,1,0:T(8,128)S(1)} fusion(bf16[4,768,1024]{2,1,0:T(8,128)(2,1)} %get-tuple-element.15, bf16[4,384,1024]{2,1,0:T(8,128)(2,1)} %all-gather.4.cloned.1.call-done), kind=kOutput, calls=%fused_computation.65 | convolution fusion | flops 2415919104 | bytes 14155776 | tf_op jit(solution)/shard_map/erh,edh->erd/dot_general | solution.py:36
  244.0 3.7 fusion
  247.7 0.3 slice_bitcast_fusion.3
  248.0 1.8 pad_maximum_fusion.1
  249.8 3.6 all-to-all-start.3
  253.4 7.3 %convert_bitcast_fusion = bf16[1,4,768,384]{3,2,1,0:T(8,128)(2,1)S(1)} fusion(bf16[4,768,1024]{2,1,0:T(8,128)(2,1)} %get-tuple-element.16, bf16[4,1024,384]{2,1,0:T(8,128)(2,1)} %all-gather.8.cloned.1.call-done), kind=kOutput, calls=%fused_computation.19 | convolution fusion | flops 2417098752 | bytes 11796480 | tf_op jit(solution)/shard_map/erh,ehd->erd/dot_general | solution.py:21
  260.7 0.3 slice_bitcast_fusion.7
  261.0 1.8 pad_maximum_fusion
  262.8 19.1 %all-to-all-done.3 = bf16[4,1,4,192,384]{4,3,2,1,0:T(8,128)(2,1)S(1)} async-done(((bf16[4,1,4,192,384]{4,3,2,1,0:T(8,128)(2,1)}), bf16[4,1,4,192,384]{4,3,2,1,0:T(8,128)(2,1)S(1)}, u32[]{:S(2)}, u32[]{:S(2)}) %all-to-all-start.3) | async-done | bytes 2359328 | tf_op jit(solution)/shard_map/all_to_all | solution.py:69
  281.8 4.7 %all-to-all-start.1 = ((bf16[4,1,4,192,384]{4,3,2,1,0:T(8,128)(2,1)}), bf16[4,1,4,192,384]{4,3,2,1,0:T(8,128)(2,1)}, u32[]{:S(2)}, u32[]{:S(2)}) async-start(bf16[4,1,4,192,384]{4,3,2,1,0:T(8,128)(2,1)} %pad_maximum_fusion), calls=%async_computation.1 | async-start | bytes 4718592 | tf_op jit(solution)/shard_map/all_to_all | solution.py:69
  286.5 2.4 convert_element_type.81
  289.0 9.0 %gather_fusion.1 = bf16[2048,384]{1,0:T(8,128)(2,1)} fusion(bf16[3072,384]{1,0:T(8,128)(2,1)S(1)} %bitcast.66, s32[2048]{0:T(1024)S(1)} %broadcast_clamp_fusion), kind=kCustom, calls=%fused_computation.1 | custom fusion | bytes 3153920 | tf_op jit(solution)/shard_map/gather | solution.py:74
  298.0 4.9 %reshape.122 = f32[1024,2,384]{2,1,0:T(2,128)} reshape(bf16[2048,384]{1,0:T(8,128)(2,1)} %gather_fusion.1) | data formatting | bytes 4718592 | tf_op jit(solution)/shard_map/convert_element_type | solution.py:75
  302.9 12.2 %all-to-all-done.1 = bf16[4,1,4,192,384]{4,3,2,1,0:T(8,128)(2,1)} async-done(((bf16[4,1,4,192,384]{4,3,2,1,0:T(8,128)(2,1)}), bf16[4,1,4,192,384]{4,3,2,1,0:T(8,128)(2,1)}, u32[]{:S(2)}, u32[]{:S(2)}) %all-to-all-start.1) | async-done | bytes 2359328 | tf_op jit(solution)/shard_map/all_to_all | solution.py:69
  315.0 9.2 %gather_fusion = bf16[2048,384]{1,0:T(8,128)(2,1)S(1)} fusion(bf16[3072,384]{1,0:T(8,128)(2,1)} %bitcast.12, s32[2048]{0:T(1024)S(1)} %broadcast_clamp_fusion), kind=kCustom, calls=%fused_computation | custom fusion | bytes 3153920 | tf_op jit(solution)/shard_map/gather | solution.py:74
  324.3 2.7 reshape.121
  327.0 10.2 %multiply_reduce_fusion = (f32[1024,2]{1,0:T(8,128)S(1)}, bf16[1024,384]{1,0:T(8,128)(2,1)}) fusion(f32[1024,2,384]{2,1,0:T(2,128)} %reshape.121, f32[1024,384]{1,0:T(8,128)} %convert_element_type.81, f32[1024,2]{1,0:T(8,128)S(1)} %copy-done.2), kind=kLoop, calls=%fused_computation.10 | loop fusion | flops 2750464 | bytes 5521408 | tf_op jit(solution)/shard_map/reduce_sum | solution.py:89
  337.2 0.8 copy.38
  338.0 5.7 %reduce_sum.96 = f32[1024,384]{1,0:T(8,128)S(1)} reduce(f32[1024,2,384]{2,1,0:T(2,128)} %reshape.122, f32[]{:T(128)} %constant.25.clone.1), dimensions={1}, to_apply=%region_9.10 | reduce | flops 393216 | bytes 4718596 | tf_op jit(solution)/shard_map/reduce_sum | solution.py:99
  343.7 0.3 fusion.11
  344.0 0.5 fusion.5
  344.5 1.7 fusion.8
  346.2 2.0 convert_element_type.90
  348.1 21.8 %reduce-scatter.6.cloned.1.call-done = bf16[4,48,1024]{2,1,0:T(8,128)(2,1)} async-done(((bf16[4,384,1024]{2,1,0:T(8,128)(2,1)}), bf16[4,48,1024]{2,1,0:T(8,128)(2,1)}) %reduce-scatter.6.cloned.1.call-update) | async-done | bytes 393232 | tf_op jit(solution)/shard_map/reduce_scatter | solution.py:110
  370.0 2.0 convert_element_type.92
  371.9 75.2 %reduce-scatter.8.cloned.1.call-done = bf16[4,128,384]{2,1,0:T(8,128)(2,1)} async-done(((bf16[4,1024,384]{2,1,0:T(8,128)(2,1)}), bf16[4,128,384]{2,1,0:T(8,128)(2,1)}) %reduce-scatter.8.cloned.1.call-update) | async-done | bytes 393232 | tf_op jit(solution)/shard_map/reduce_scatter | solution.py:113
  447.1 1.9 convert_element_type.94
  (41 shorter events, 1.2 us)
Async XLA Ops:
  7.2 8.7 %copy-start = (bf16[1024,384]{1,0:T(8,128)(2,1)S(1)}, bf16[1024,384]{1,0:T(8,128)(2,1)}, u32[]{:S(2)}) copy-start(bf16[1024,384]{1,0:T(8,128)(2,1)} %param.8) | copy-start | bytes 2359300
  7.2 9.4 %copy-start.6 = (f32[384]{0:T(512)S(1)}, f32[384]{0:T(512)}, u32[]{:S(2)}) copy-start(f32[384]{0:T(512)} %param.9) | copy-start | bytes 4612
  7.2 95.4 %all-gather.4.cloned.1.call-start = ((), (), s32[]{:S(2)}) async-start(), calls=%async_computation.7 | async-start | bytes 3538944 | tf_op jit(solution)/shard_map/all_gather | solution.py:78
  7.9 126.0 %all-gather.6.cloned.1.call-start = ((), (), s32[]{:S(2)}) async-start(), calls=%async_computation.8 | async-start | bytes 3538944 | tf_op jit(solution)/shard_map/all_gather | solution.py:79
  8.7 186.1 %all-gather.8.cloned.1.call-start = ((), (), s32[]{:S(2)}) async-start(), calls=%async_computation.9 | async-start | bytes 3538944 | tf_op jit(solution)/shard_map/all_gather | solution.py:80
  10.3 6.5 %copy-start.5 = (s32[1024,2]{0,1:T(2,128)S(1)}, s32[1024,2]{0,1:T(2,128)}, u32[]{:S(2)}) copy-start(s32[1024,2]{0,1:T(2,128)} %param.10) | copy-start | bytes 24580
  31.7 4.5 copy-start.7
  31.7 33.1 %all-to-all-start = ((bf16[4,4,192,384]{3,2,1,0:T(8,128)(2,1)}), bf16[4,4,192,384]{3,2,1,0:T(8,128)(2,1)S(1)}, u32[]{:S(2)}, u32[]{:S(2)}) async-start(bf16[4,4,192,384]{3,2,1,0:T(8,128)(2,1)} %bitcast.73), calls=%async_computation | async-start | bytes 4718592 | tf_op jit(solution)/shard_map/all_to_all | solution.py:64
  64.8 1.4 copy-start.1
  66.2 33.0 %all-to-all-start.2 = ((bf16[4,4,192,384]{3,2,1,0:T(8,128)(2,1)}), bf16[4,4,192,384]{3,2,1,0:T(8,128)(2,1)}, u32[]{:S(2)}, u32[]{:S(2)}) async-start(bf16[4,4,192,384]{3,2,1,0:T(8,128)(2,1)} %bitcast.72), calls=%async_computation.2 | async-start | bytes 4718592 | tf_op jit(solution)/shard_map/all_to_all | solution.py:64
  70.7 275.5 %reduce-scatter.4.cloned.1.call-start = ((), (), s32[]{:S(2)}) async-start(), calls=%async_computation.10 | async-start | bytes 3538944 | tf_op jit(solution)/shard_map/reduce_scatter | solution.py:107
  219.9 150.0 %reduce-scatter.6.cloned.1.call-start = ((), (), s32[]{:S(2)}) async-start(), calls=%async_computation.11 | async-start | bytes 3538944 | tf_op jit(solution)/shard_map/reduce_scatter | solution.py:110
  227.5 1.7 copy-start.4
  227.6 219.6 %reduce-scatter.8.cloned.1.call-start = ((), (), s32[]{:S(2)}) async-start(), calls=%async_computation.12 | async-start | bytes 3538944 | tf_op jit(solution)/shard_map/reduce_scatter | solution.py:113
  237.2 6.8 %slice-start = ((s8[6291456]{0:T(1024)(128)(4,1)}), s8[2097152]{0:T(1024)(128)(4,1)S(1)}, s32[]{:S(2)}) async-start(s8[6291456]{0:T(1024)(128)(4,1)} %bitcast.82), calls=%async_computation.13 | async-start | bytes 4194304
  237.2 6.7 %copy-start.3 = (bf16[4,384,1024]{2,1,0:T(8,128)(2,1)S(1)}, bf16[4,384,1024]{2,1,0:T(8,128)(2,1)}, u32[]{:S(2)}) copy-start(bf16[4,384,1024]{2,1,0:T(8,128)(2,1)} %all-gather.6.cloned.1.call-done) | copy-start | bytes 9437188
  237.2 6.8 %slice-start.1 = ((s8[6291456]{0:T(1024)(128)(4,1)}), s8[4194304]{0:T(1024)(128)(4,1)S(1)}, s32[]{:S(2)}) async-start(s8[6291456]{0:T(1024)(128)(4,1)} %bitcast.82), calls=%async_computation.14 | async-start | bytes 8388608
  249.8 32.1 %all-to-all-start.3 = ((bf16[4,1,4,192,384]{4,3,2,1,0:T(8,128)(2,1)}), bf16[4,1,4,192,384]{4,3,2,1,0:T(8,128)(2,1)S(1)}, u32[]{:S(2)}, u32[]{:S(2)}) async-start(bf16[4,1,4,192,384]{4,3,2,1,0:T(8,128)(2,1)} %pad_maximum_fusion.1), calls=%async_computation.3 | async-start | bytes 4718592 | tf_op jit(solution)/shard_map/all_to_all | solution.py:69
  281.8 33.2 %all-to-all-start.1 = ((bf16[4,1,4,192,384]{4,3,2,1,0:T(8,128)(2,1)}), bf16[4,1,4,192,384]{4,3,2,1,0:T(8,128)(2,1)}, u32[]{:S(2)}, u32[]{:S(2)}) async-start(bf16[4,1,4,192,384]{4,3,2,1,0:T(8,128)(2,1)} %pad_maximum_fusion), calls=%async_computation.1 | async-start | bytes 4718592 | tf_op jit(solution)/shard_map/all_to_all | solution.py:69
  324.2 2.7 copy-start.2
Sparse Core Ops, SparseCore 0:
  10.2 62.7 all-gather.3
  75.2 58.6 all-gather.5
  136.1 58.6 all-gather.7
  220.1 72.9 reduce-scatter.3
  296.5 73.4 reduce-scatter.5
  373.4 73.6 reduce-scatter.7
